TPU v7x, 32 devices: a whole 2x2x4 slice. The times are simulated.
32 devices in a mesh: segment: 8 (over y, x, core), head: 4 (over z).
Axes of the slice: x: 2, y: 2, z: 4, core: 2. Of those that a mesh axis runs over, the one named last changes fastest.
Arguments:
- grad_in: float32 [8, 128, 512], P('segment'), may hold values from -6 to 6
- memory: bfloat16 [8, 128, 512], P('segment'), may hold values from -120 to 120
- enc_grad_in: float32 [8, 128, 512], P('segment', None, 'head'), may hold values from -3 to 3
- act_stash: bfloat16 [8, 3, 128, 512], P('segment'), may hold values from -120 to 120
- slot_order: int32 [8, 3], P('segment'), may hold values from 0 to 2, each once within a row
- lengths: int32 [8, 3], P('segment'), may hold values from 16 to 128, as said below
- w_query: bfloat16 [8, 512, 4096], P('segment', None, 'head'), may hold values from -0.0234375 to 0.0234375
- w_key: bfloat16 [8, 512, 4096], P('segment', None, 'head'), may hold values from -0.25 to 0.25
- w_value: bfloat16 [8, 512, 4096], P('segment', None, 'head'), may hold values from -0.25 to 0.25
- w_out: bfloat16 [8, 4096, 512], P('segment', 'head'), may hold values from -0.09375 to 0.09375
Outputs:
- grad_out: float32 [8, 128, 512], P('segment')
- enc_grad_out: float32 [8, 128, 512], P('segment', None, 'head')
Inputs may be any that keep to these rules, and one draw needn't show every extreme that they name: `slot_order`: each row lists every stash slot once. `lengths`: some entry equals 128.
All inputs are finite; a program needn't handle non-finite values.
Results may differ from a plain program's by a relative error of at most 0.018.
The roundings to bfloat16 on the way count: a program that leaves them out, or rounds other values in their place, can miss the bound.
Values may be sent and summed in bfloat16 or wider, within the bound.
No kernel may reach another device: no remote copies, remote signals or barrier semaphores. Data moves between devices by JAX's collectives and lax.ppermute only.
A program may use at most 64 MiB of HBM per device.

v0:
```python
import jax
import jax.numpy as jnp
from jax import lax
from jax.sharding import PartitionSpec as P

HEAD_DIM = 128
TICKS = 3


def shifted(value, axis, steps):
    count = lax.axis_size(axis)
    pairs = [(source, (source + steps) % count) for source in range(count)]
    return lax.ppermute(value, axis, pairs)


def local_terms(
    gradient_low, held, decoded, length, query_weight, key_weight, value_weight, out_weight
):
    inner = query_weight.shape[1]
    head_local = inner // HEAD_DIM
    dec_rows = decoded.shape[0]
    enc_rows = held.shape[0]
    queries = jnp.dot(decoded, query_weight, preferred_element_type=jnp.float32).astype(
        jnp.bfloat16
    )
    keys = jnp.dot(held, key_weight, preferred_element_type=jnp.float32).astype(jnp.bfloat16)
    values = jnp.dot(held, value_weight, preferred_element_type=jnp.float32).astype(jnp.bfloat16)
    query_heads = queries.reshape(dec_rows, head_local, HEAD_DIM)
    key_heads = keys.reshape(enc_rows, head_local, HEAD_DIM)
    value_heads = values.reshape(enc_rows, head_local, HEAD_DIM)
    scores = jnp.einsum("qhd,khd->hqk", query_heads, key_heads, preferred_element_type=jnp.float32)
    allowed = lax.broadcasted_iota(jnp.int32, (1, 1, enc_rows), 2) < length
    scores = jnp.where(allowed, scores, jnp.float32(-1e30))
    row_max = jnp.max(scores, axis=-1, keepdims=True)
    expo = jnp.exp(scores - row_max)
    attention = expo / jnp.sum(expo, axis=-1, keepdims=True)
    attention_low = attention.astype(jnp.bfloat16)
    context_grad = jnp.einsum(
        "qe,ie->qi", gradient_low, out_weight, preferred_element_type=jnp.float32
    ).astype(jnp.bfloat16)
    context_heads = context_grad.reshape(dec_rows, head_local, HEAD_DIM)
    prob_grad = jnp.einsum(
        "qhd,khd->hqk", context_heads, value_heads, preferred_element_type=jnp.float32
    )
    score_grad = (
        attention * (prob_grad - jnp.sum(attention * prob_grad, axis=-1, keepdims=True))
    ).astype(jnp.bfloat16)
    query_grad = (
        jnp.einsum("hqk,khd->qhd", score_grad, key_heads, preferred_element_type=jnp.float32)
        .astype(jnp.bfloat16)
        .reshape(dec_rows, inner)
    )
    key_grad = (
        jnp.einsum("hqk,qhd->khd", score_grad, query_heads, preferred_element_type=jnp.float32)
        .astype(jnp.bfloat16)
        .reshape(enc_rows, inner)
    )
    value_grad = (
        jnp.einsum("hqk,qhd->khd", attention_low, context_heads, preferred_element_type=jnp.float32)
        .astype(jnp.bfloat16)
        .reshape(enc_rows, inner)
    )
    decoder_part = jnp.einsum(
        "qi,ei->qe", query_grad, query_weight, preferred_element_type=jnp.float32
    )
    memory_part = jnp.einsum("ki,ei->ke", key_grad, key_weight, preferred_element_type=jnp.float32)
    memory_part = memory_part + jnp.einsum(
        "ki,ei->ke", value_grad, value_weight, preferred_element_type=jnp.float32
    )
    return (decoder_part, memory_part)


def body(
    grad_in, memory, enc_grad_in, act_stash, slot_order, lengths, w_query, w_key, w_value, w_out
):
    held = memory[0]
    stash_local = act_stash[0]
    order_row = slot_order[0]
    length_row = lengths[0]
    head_count = lax.axis_size("head")
    shard_width = enc_grad_in.shape[2]
    feature_share = grad_in.shape[2] // head_count
    gradient = lax.dynamic_slice_in_dim(
        grad_in[0], lax.axis_index("head") * feature_share, feature_share, 1
    )
    carried = jnp.zeros((held.shape[0], shard_width * head_count), jnp.float32)
    carried = lax.dynamic_update_slice_in_dim(
        carried, enc_grad_in[0], lax.axis_index("head") * shard_width, 1
    )
    for tick_index in range(TICKS):
        if tick_index == 0:
            gradient_low = grad_in[0].astype(jnp.bfloat16)
        else:
            gradient_low = lax.all_gather(gradient.astype(jnp.bfloat16), "head", axis=1, tiled=True)
        decoded = lax.dynamic_index_in_dim(stash_local, order_row[tick_index], 0, keepdims=False)
        decoder_part, memory_part = local_terms(
            gradient_low,
            held,
            decoded,
            length_row[tick_index],
            w_query[0],
            w_key[0],
            w_value[0],
            w_out[0],
        )
        gradient = gradient + lax.psum_scatter(
            decoder_part, "head", scatter_dimension=1, tiled=True
        )
        carried = carried + memory_part
        gradient, carried = shifted((gradient, carried), "segment", -1)
        if tick_index + 1 < TICKS:
            held = shifted(held, "segment", -1)
    carried = lax.psum_scatter(carried, "head", scatter_dimension=1, tiled=True)
    gradient = lax.all_gather(gradient, "head", axis=1, tiled=True)
    return (gradient[None], carried[None])


def solution(mesh):
    in_specs = (
        P("segment", None, None),
        P("segment", None, None),
        P("segment", None, "head"),
        P("segment", None, None, None),
        P("segment", None),
        P("segment", None),
        P("segment", None, "head"),
        P("segment", None, "head"),
        P("segment", None, "head"),
        P("segment", "head", None),
    )
    out_specs = (P("segment", None, None), P("segment", None, "head"))
    return jax.shard_map(body, mesh=mesh, in_specs=in_specs, out_specs=out_specs, check_vma=False)
```

profile of v0, /device:TPU:0, one launch (start us, length us, event | category | flops | bytes accessed | tf_op | source)
XLA Modules:
  0.0 184.4 jit_solution(5758655735363486501)
XLA Ops:
  7.2 3.4 %collective-permute-start.1 = (bf16[128,512]{1,0:T(8,128)(2,1)}, bf16[128,512]{1,0:T(8,128)(2,1)}, u32[]{:S(2)}, u32[]{:S(2)}) collective-permute-start(bf16[128,512]{1,0:T(8,128)(2,1)} %bitcast.204), channel_id=1, source_target_pairs={{0,28},{4,0},{8,4},{12,8},{16,12},{20,16},{24,20},{28,24},{1,29},{... | collective-permute-start | bytes 393224 | tf_op jit(solution)/shard_map/ppermute | solution.py:13
  12.6 1.4 fusion.66
  15.2 1.2 convolution_convert_fusion.19
  16.7 2.2 %convolution_convert_fusion.18 = bf16[128,1024]{1,0:T(8,128)(2,1)} fusion(bf16[1,1024,512]{2,1,0:T(8,128)(2,1)S(1)} %copy-done.3, f32[1,128,512]{2,1,0:T(8,128)} %param.10), kind=kOutput, calls=%fused_computation.30 | convolution fusion | flops 134414336 | bytes 1572864 | tf_op jit(solution)/shard_map/qe,ie->qi/dot_general | solution.py:38
  18.9 1.8 copy.53
  20.8 1.0 convolution_convert_fusion.20
  21.8 1.8 copy.51
  24.6 2.1 %fusion.68 = (f32[8,128]{1,0:T(8,128)S(1)}, f32[8,128,128]{1,2,0:T(8,128)}) fusion(bf16[128,8,128]{0,2,1:T(8,128)(2,1)S(1)} %bitcast.191, bf16[128,8,128]{0,2,1:T(8,128)(2,1)} %bitcast.194, pred[128]{0:T(512)(128)(4,1)S(1)} %iota_compare_fusion.2), kind=kOutput, calls=%fused_computation.109 | convolution fusion | flops 33947776 | bytes 1052800 | tf_op jit(solution)/shard_map/sub | solution.py:35
  26.7 1.5 multiply_reduce_fusion.2
  29.3 1.2 fusion.28
  30.6 2.3 %convolution_convert_fusion.4 = bf16[8,128,128]{2,1,0:T(8,128)(2,1)} fusion(bf16[128,8,128]{0,2,1:T(8,128)(2,1)} %bitcast.208, f32[8,128]{1,0:T(8,128)S(1)} %get-tuple-element.8, bf16[128,8,128]{0,2,1:T(8,128)(2,1)} %bitcast.192, bf16[128,8,128]{0,2,1:T(8,128)(2,1)} %bitcast.195, pred[128]{0:T(512)(128)(4,1)S(1)} %iota_compare_fusion.2), kind=kOutput, calls=%fused_computation.16 | convolution fusion | flops 67765376 | bytes 1052800 | tf_op jit(solution)/shard_map/hqk,qhd->khd/dot_general | solution.py:59
  33.0 2.0 %convolution_convert_fusion.5 = bf16[8,128,128]{2,1,0:T(8,128)(2,1)} fusion(bf16[128,8,128]{0,2,1:T(8,128)(2,1)} %bitcast.193, bf16[8,128,128]{1,2,0:T(8,128)(2,1)S(1)} %multiply_convert_fusion.2), kind=kOutput, calls=%fused_computation.17 | convolution fusion | flops 33685504 | bytes 786432 | tf_op jit(solution)/shard_map/hqk,qhd->khd/dot_general | solution.py:54
  34.9 1.4 fusion.35
  36.4 2.2 %convolution_add_fusion.2 = f32[128,512]{1,0:T(8,128)} fusion(f32[128,512]{1,0:T(8,128)S(1)} %fusion.35, bf16[128,1024]{0,1:T(8,128)(2,1)} %bitcast.206, bf16[1,512,1024]{2,1,0:T(8,128)(2,1)S(1)} %copy-done.2), kind=kOutput, calls=%fused_computation.39 | convolution fusion | flops 134283264 | bytes 1835008 | tf_op jit(solution)/shard_map/ki,ei->ke/dot_general | solution.py:67
  38.6 1.5 fusion.60
  43.9 1.9 %convolution_convert_fusion.9 = bf16[128,1024]{1,0:T(8,128)(2,1)} fusion(bf16[1,512,1024]{2,1,0:T(8,128)(2,1)S(1)} %copy-done, bf16[1,3,128,512]{3,2,1,0:T(8,128)(2,1)} %param.13, s32[]{:T(128)S(6)} %select_n.29), kind=kOutput, calls=%fused_computation.21 | convolution fusion | flops 134348800 | bytes 1441796 | tf_op jit(solution)/shard_map/dot_general | solution.py:23
  46.5 1.9 %convolution_convert_fusion.14 = bf16[128,1024]{1,0:T(8,128)(2,1)} fusion(bf16[1,512,1024]{2,1,0:T(8,128)(2,1)S(1)} %copy-done, bf16[1,3,128,512]{3,2,1,0:T(8,128)(2,1)} %param.13, s32[]{:T(128)S(6)} %select_n.27), kind=kOutput, calls=%fused_computation.26 | convolution fusion | flops 134348800 | bytes 1441796 | tf_op jit(solution)/shard_map/dot_general | solution.py:23
  49.0 1.1 copy.58
  50.2 1.9 %copy.55 = bf16[128,1024]{0,1:T(8,128)(2,1)} copy(bf16[128,1024]{1,0:T(8,128)(2,1)} %convolution_convert_fusion.14) | data formatting | bytes 524288 | tf_op jit(solution)/shard_map/reshape | solution.py:28
  52.7 1.9 %convolution_convert_fusion.15 = bf16[128,1024]{1,0:T(8,128)(2,1)} fusion(bf16[128,512]{1,0:T(8,128)(2,1)} %collective-permute-done.1, bf16[1,512,1024]{2,1,0:T(8,128)(2,1)S(1)} %copy-done.1), kind=kOutput, calls=%fused_computation.27 | convolution fusion | flops 134348800 | bytes 1441792 | tf_op jit(solution)/shard_map/dot_general | solution.py:26
  54.7 1.8 copy.54
  56.5 2.2 %fusion.69 = (f32[8,128]{1,0:T(8,128)S(1)}, f32[8,128,128]{1,2,0:T(8,128)}) fusion(bf16[128,8,128]{0,2,1:T(8,128)(2,1)} %bitcast.185, bf16[128,8,128]{0,2,1:T(8,128)(2,1)} %bitcast.188, pred[128]{0:T(512)(128)(4,1)S(1)} %iota_compare_fusion.1), kind=kOutput, calls=%fused_computation.110 | convolution fusion | flops 33947776 | bytes 1052800 | tf_op jit(solution)/shard_map/sub | solution.py:35
  59.3 2.0 %fusion.10 = bf16[16,8,8,128]{3,2,1,0:T(8,128)(2,1)} fusion(bf16[128,512]{1,0:T(8,128)(2,1)} %collective-permute-done.1, bf16[1,512,1024]{2,1,0:T(8,128)(2,1)S(1)} %copy-done.2), kind=kOutput, calls=%fused_computation.34 | convolution fusion | flops 134348800 | bytes 1441792 | tf_op jit(solution)/shard_map/dot_general | solution.py:27
  62.1 1.0 convolution_convert_fusion.10
  63.1 1.8 copy.57
  64.9 2.1 %fusion.70 = (f32[8,128]{1,0:T(8,128)S(1)}, f32[8,128,128]{1,2,0:T(8,128)}) fusion(bf16[128,8,128]{0,2,1:T(8,128)(2,1)S(1)} %bitcast.179, bf16[128,8,128]{0,2,1:T(8,128)(2,1)} %bitcast.182, pred[128]{0:T(512)(128)(4,1)S(1)} %iota_compare_fusion), kind=kOutput, calls=%fused_computation.111 | convolution fusion | flops 33947776 | bytes 1052800 | tf_op jit(solution)/shard_map/sub | solution.py:35
  68.0 2.7 %collective-permute-start = (f32[128,128]{1,0:T(8,128)S(1)}, f32[128,128]{1,0:T(8,128)S(1)}, u32[]{:S(2)}, u32[]{:S(2)}) collective-permute-start(f32[128,128]{1,0:T(8,128)S(1)} %bitcast_add_fusion.1), channel_id=1, source_target_pairs={{0,28},{4,0},{8,4},{12,8},{16,12},{20,16},{24,20},{28,24},{1,29},{... | collective-permute-start | bytes 196616 | tf_op jit(solution)/shard_map/ppermute | solution.py:13
  70.7 1.0 fusion.11
  73.2 12.5 %all_gather.9 = bf16[128,512]{1,0:T(8,128)(2,1)S(1)} all-gather(bf16[128,128]{1,0:T(8,128)(2,1)S(1)} %convert_element_type.131), channel_id=1, replica_groups=mesh['segment'=8,'head'=4] {'head'}, dimensions={1}, use_global_device_ids=true | all-gather | bytes 163840 | tf_op jit(solution)/shard_map/all_gather | solution.py:94
  87.0 1.5 multiply_reduce_fusion.1
  89.7 1.2 fusion.25
  91.0 2.4 %convolution_convert_fusion.2 = bf16[8,128,128]{2,1,0:T(8,128)(2,1)} fusion(bf16[128,8,128]{0,2,1:T(8,128)(2,1)} %bitcast.210, f32[8,128]{1,0:T(8,128)S(1)} %get-tuple-element.12, bf16[128,8,128]{0,2,1:T(8,128)(2,1)} %bitcast.186, bf16[128,8,128]{0,2,1:T(8,128)(2,1)} %bitcast.189, pred[128]{0:T(512)(128)(4,1)S(1)} %iota_compare_fusion.1), kind=kOutput, calls=%fused_computation.14 | convolution fusion | flops 67765376 | bytes 1052800 | tf_op jit(solution)/shard_map/hqk,qhd->khd/dot_general | solution.py:59
  93.3 1.2 convolution_convert_fusion.3
  95.1 14.4 %reduce-scatter.7.cloned.1.call-done = f32[128,128]{1,0:T(8,128)} async-done(((f32[128,512]{1,0:T(8,128)}), f32[128,128]{1,0:T(8,128)}) %reduce-scatter.7.cloned.1.call-update) | async-done | bytes 65552 | tf_op jit(solution)/shard_map/reduce_scatter | solution.py:106
  110.5 2.3 %fusion.12 = f32[128,512]{1,0:T(8,128)} fusion(f32[128,512]{1,0:T(8,128)} %collective-permute-done.5, f32[128,512]{1,0:T(8,128)S(1)} %fusion.33, bf16[128,1024]{0,1:T(8,128)(2,1)} %bitcast.213, bf16[1,512,1024]{2,1,0:T(8,128)(2,1)S(1)} %copy-done.2), kind=kOutput, calls=%fused_computation.38 | convolution fusion | flops 134348800 | bytes 2097152 | tf_op jit(solution)/shard_map/ki,ei->ke/dot_general | solution.py:67
  112.8 2.4 %collective-permute-start.6 = (f32[128,512]{1,0:T(8,128)}, f32[128,512]{1,0:T(8,128)}, u32[]{:S(2)}, u32[]{:S(2)}) collective-permute-start(f32[128,512]{1,0:T(8,128)} %fusion.12), channel_id=1, source_target_pairs={{0,28},{4,0},{8,4},{12,8},{16,12},{20,16},{24,20},{28,24},{1,29},{... | collective-permute-start | bytes 786440 | tf_op jit(solution)/shard_map/ppermute | solution.py:13
  115.2 12.3 %all_gather.10 = bf16[128,512]{1,0:T(8,128)(2,1)S(1)} all-gather(bf16[128,128]{1,0:T(8,128)(2,1)S(1)} %convert_element_type.139), channel_id=1, replica_groups=mesh['segment'=8,'head'=4] {'head'}, dimensions={1}, use_global_device_ids=true | all-gather | bytes 163840 | tf_op jit(solution)/shard_map/all_gather | solution.py:94
  127.5 1.2 convolution_convert_fusion.8
  128.7 1.8 copy.59
  130.5 2.3 %convolution_convert_fusion = bf16[8,128,128]{2,1,0:T(8,128)(2,1)} fusion(bf16[128,8,128]{0,2,1:T(8,128)(2,1)} %bitcast.211, f32[8,128]{1,0:T(8,128)S(1)} %get-tuple-element.16, bf16[128,8,128]{0,2,1:T(8,128)(2,1)S(1)} %bitcast.180, bf16[128,8,128]{0,2,1:T(8,128)(2,1)} %bitcast.183, pred[128]{0:T(512)(128)(4,1)S(1)} %iota_compare_fusion), kind=kOutput, calls=%fused_computation.12 | convolution fusion | flops 67765376 | bytes 1052800 | tf_op jit(solution)/shard_map/hqk,qhd->khd/dot_general | solution.py:59
  132.8 1.5 multiply_reduce_fusion
  135.6 1.2 fusion.22
  136.8 1.4 fusion.31
  140.7 3.9 %collective-permute-done.7 = f32[128,512]{1,0:T(8,128)S(1)} collective-permute-done((f32[128,512]{1,0:T(8,128)S(1)}, f32[128,512]{1,0:T(8,128)S(1)}, u32[]{:S(2)}, u32[]{:S(2)}) %collective-permute-start.7) | collective-permute-done | bytes 262176 | tf_op jit(solution)/shard_map/ppermute | solution.py:13
  145.3 9.7 %reduce-scatter.9.cloned.1.call-done = f32[128,128]{1,0:T(8,128)} async-done(((f32[128,512]{1,0:T(8,128)}), f32[128,128]{1,0:T(8,128)}) %reduce-scatter.9.cloned.1.call-update) | async-done | bytes 65552 | tf_op jit(solution)/shard_map/reduce_scatter | solution.py:106
  155.9 1.9 %collective-permute-done.4 = f32[128,128]{1,0:T(8,128)S(1)} collective-permute-done((f32[128,128]{1,0:T(8,128)S(1)}, f32[128,128]{1,0:T(8,128)S(1)}, u32[]{:S(2)}, u32[]{:S(2)}) %collective-permute-start.4) | collective-permute-done | bytes 65568 | tf_op jit(solution)/shard_map/ppermute | solution.py:13
  157.8 14.7 %all_gather.11 = f32[128,512]{1,0:T(8,128)S(1)} all-gather(f32[128,128]{1,0:T(8,128)S(1)} %collective-permute-done.4), channel_id=1, replica_groups=mesh['segment'=8,'head'=4] {'head'}, dimensions={1}, use_global_device_ids=true | all-gather | bytes 327680 | tf_op jit(solution)/shard_map/all_gather | solution.py:114
  172.5 4.6 %reduce-scatter.11.cloned.1.call-done = f32[128,128]{1,0:T(8,128)} async-done(((f32[128,512]{1,0:T(8,128)}), f32[128,128]{1,0:T(8,128)}) %reduce-scatter.11.cloned.1.call-update) | async-done | bytes 65552 | tf_op jit(solution)/shard_map/reduce_scatter | solution.py:113
  (88 shorter events, 19.6 us)
Async XLA Ops:
  7.2 8.1 %copy-start = (bf16[1,512,1024]{2,1,0:T(8,128)(2,1)S(1)}, bf16[1,512,1024]{2,1,0:T(8,128)(2,1)}, u32[]{:S(2)}) copy-start(bf16[1,512,1024]{2,1,0:T(8,128)(2,1)} %param.16) | copy-start | bytes 3145732
  7.2 3.5 %copy-start.21 = (s32[1,3]{1,0:T(1,128)S(1)}, s32[1,3]{1,0:T(1,128)}, u32[]{:S(2)}) copy-start(s32[1,3]{1,0:T(1,128)} %param.14) | copy-start | bytes 40
  7.2 9.5 %copy-start.3 = (bf16[1,1024,512]{2,1,0:T(8,128)(2,1)S(1)}, bf16[1,1024,512]{2,1,0:T(8,128)(2,1)}, u32[]{:S(2)}) copy-start(bf16[1,1024,512]{2,1,0:T(8,128)(2,1)} %param.19) | copy-start | bytes 3145732
  7.2 59.8 %reduce-scatter.5.cloned.1.call-start = ((), (), s32[]{:S(2)}) async-start(), calls=%async_computation.4 | async-start | bytes 327680 | tf_op jit(solution)/shard_map/reduce_scatter | solution.py:106
  7.2 45.5 %collective-permute-start.1 = (bf16[128,512]{1,0:T(8,128)(2,1)}, bf16[128,512]{1,0:T(8,128)(2,1)}, u32[]{:S(2)}, u32[]{:S(2)}) collective-permute-start(bf16[128,512]{1,0:T(8,128)(2,1)} %bitcast.204), channel_id=1, source_target_pairs={{0,28},{4,0},{8,4},{12,8},{16,12},{20,16},{24,20},{28,24},{1,29},{... | collective-permute-start | bytes 393224 | tf_op jit(solution)/shard_map/ppermute | solution.py:13
  16.7 7.9 %copy-start.10 = (bf16[128,1024]{0,1:T(8,128)(2,1)}, bf16[128,1024]{0,1:T(8,128)(2,1)S(1)}, u32[]{:S(2)}) copy-start(bf16[128,1024]{0,1:T(8,128)(2,1)S(1)} %copy.52) | copy-start | bytes 786436
  16.7 4.1 %copy-start.1 = (bf16[1,512,1024]{2,1,0:T(8,128)(2,1)S(1)}, bf16[1,512,1024]{2,1,0:T(8,128)(2,1)}, u32[]{:S(2)}) copy-start(bf16[1,512,1024]{2,1,0:T(8,128)(2,1)} %param.17) | copy-start | bytes 3145732
  18.9 1.8 copy-start.15
  20.7 2.8 %copy-start.2 = (bf16[1,512,1024]{2,1,0:T(8,128)(2,1)S(1)}, bf16[1,512,1024]{2,1,0:T(8,128)(2,1)}, u32[]{:S(2)}) copy-start(bf16[1,512,1024]{2,1,0:T(8,128)(2,1)} %param.18) | copy-start | bytes 3145732
  26.7 1.5 copy-start.14
  28.2 1.0 copy-start.11
  30.6 79.0 %reduce-scatter.7.cloned.1.call-start = ((), (), s32[]{:S(2)}) async-start(), calls=%async_computation.5 | async-start | bytes 327680 | tf_op jit(solution)/shard_map/reduce_scatter | solution.py:106
  36.4 2.2 %copy-start.20 = (f32[1,128,128]{2,1,0:T(8,128)S(1)}, f32[1,128,128]{2,1,0:T(8,128)}, u32[]{:S(2)}) copy-start(f32[1,128,128]{2,1,0:T(8,128)} %param.12) | copy-start | bytes 196612
  40.0 70.4 %collective-permute-start.5 = (f32[128,512]{1,0:T(8,128)}, f32[128,512]{1,0:T(8,128)}, u32[]{:S(2)}, u32[]{:S(2)}) collective-permute-start(f32[128,512]{1,0:T(8,128)} %fusion.60), channel_id=1, source_target_pairs={{0,28},{4,0},{8,4},{12,8},{16,12},{20,16},{24,20},{28,24},{1,29},{... | collective-permute-start | bytes 786440 | tf_op jit(solution)/shard_map/ppermute | solution.py:13
  50.2 14.8 %copy-start.6 = (bf16[128,1024]{0,1:T(8,128)(2,1)}, bf16[128,1024]{0,1:T(8,128)(2,1)S(1)}, u32[]{:S(2)}) copy-start(bf16[128,1024]{0,1:T(8,128)(2,1)S(1)} %copy.58) | copy-start | bytes 786436
  58.6 3.5 %collective-permute-start.3 = (bf16[128,512]{1,0:T(8,128)(2,1)}, bf16[128,512]{1,0:T(8,128)(2,1)S(1)}, u32[]{:S(2)}, u32[]{:S(2)}) collective-permute-start(bf16[128,512]{1,0:T(8,128)(2,1)} %collective-permute-done.1), channel_id=1, source_target_pairs={{0,28},{4,0},{8,4},{12,8},{16,12},{20,16},{24,20},{28,24},{1,29},{... | collective-permute-start | bytes 393224 | tf_op jit(solution)/shard_map/ppermute | solution.py:13
  67.0 18.7 %copy-start.4 = (bf16[1,1024,512]{2,1,0:T(8,128)(2,1)S(1)}, bf16[1,1024,512]{2,1,0:T(8,128)(2,1)}, u32[]{:S(2)}) copy-start(bf16[1,1024,512]{2,1,0:T(8,128)(2,1)} %param.19) | copy-start | bytes 3145732
  68.0 4.6 %collective-permute-start = (f32[128,128]{1,0:T(8,128)S(1)}, f32[128,128]{1,0:T(8,128)S(1)}, u32[]{:S(2)}, u32[]{:S(2)}) collective-permute-start(f32[128,128]{1,0:T(8,128)S(1)} %bitcast_add_fusion.1), channel_id=1, source_target_pairs={{0,28},{4,0},{8,4},{12,8},{16,12},{20,16},{24,20},{28,24},{1,29},{... | collective-permute-start | bytes 196616 | tf_op jit(solution)/shard_map/ppermute | solution.py:13
  72.6 0.6 copy-start.17
  87.0 1.5 copy-start.13
  88.5 1.0 copy-start.9
  90.9 64.1 %reduce-scatter.9.cloned.1.call-start = ((), (), s32[]{:S(2)}) async-start(), calls=%async_computation.6 | async-start | bytes 327680 | tf_op jit(solution)/shard_map/reduce_scatter | solution.py:106
  94.6 14.9 %copy-start.18 = (f32[128,128]{1,0:T(8,128)S(1)}, f32[128,128]{1,0:T(8,128)}, u32[]{:S(2)}) copy-start(f32[128,128]{1,0:T(8,128)} %copy-done.17) | copy-start | bytes 196612
  110.4 4.8 %collective-permute-start.2 = (f32[128,128]{1,0:T(8,128)S(1)}, f32[128,128]{1,0:T(8,128)S(1)}, u32[]{:S(2)}, u32[]{:S(2)}) collective-permute-start(f32[128,128]{1,0:T(8,128)S(1)} %add.56), channel_id=1, source_target_pairs={{0,28},{4,0},{8,4},{12,8},{16,12},{20,16},{24,20},{28,24},{1,29},{... | collective-permute-start | bytes 196616 | tf_op jit(solution)/shard_map/ppermute | solution.py:13
  110.5 17.0 %copy-start.5 = (bf16[1,1024,512]{2,1,0:T(8,128)(2,1)S(1)}, bf16[1,1024,512]{2,1,0:T(8,128)(2,1)}, u32[]{:S(2)}) copy-start(bf16[1,1024,512]{2,1,0:T(8,128)(2,1)} %param.19) | copy-start | bytes 3145732
  112.8 26.9 %collective-permute-start.6 = (f32[128,512]{1,0:T(8,128)}, f32[128,512]{1,0:T(8,128)}, u32[]{:S(2)}, u32[]{:S(2)}) collective-permute-start(f32[128,512]{1,0:T(8,128)} %fusion.12), channel_id=1, source_target_pairs={{0,28},{4,0},{8,4},{12,8},{16,12},{20,16},{24,20},{28,24},{1,29},{... | collective-permute-start | bytes 786440 | tf_op jit(solution)/shard_map/ppermute | solution.py:13
  128.7 1.8 copy-start.7
  132.8 1.5 copy-start.12
  134.4 1.0 copy-start.8
  138.2 1.0 copy-start.16
  138.3 38.9 %reduce-scatter.11.cloned.1.call-start = ((), (), s32[]{:S(2)}) async-start(), calls=%async_computation.7 | async-start | bytes 327680 | tf_op jit(solution)/shard_map/reduce_scatter | solution.py:113
  140.7 3.9 %collective-permute-start.7 = (f32[128,512]{1,0:T(8,128)S(1)}, f32[128,512]{1,0:T(8,128)S(1)}, u32[]{:S(2)}, u32[]{:S(2)}) collective-permute-start(f32[128,512]{1,0:T(8,128)S(1)} %add.65), channel_id=1, source_target_pairs={{0,28},{4,0},{8,4},{12,8},{16,12},{20,16},{24,20},{28,24},{1,29},{... | collective-permute-start | bytes 786440 | tf_op jit(solution)/shard_map/ppermute | solution.py:13
  144.6 0.7 copy-start.19
  155.9 2.0 %collective-permute-start.4 = (f32[128,128]{1,0:T(8,128)S(1)}, f32[128,128]{1,0:T(8,128)S(1)}, u32[]{:S(2)}, u32[]{:S(2)}) collective-permute-start(f32[128,128]{1,0:T(8,128)S(1)} %add.58), channel_id=1, source_target_pairs={{0,28},{4,0},{8,4},{12,8},{16,12},{20,16},{24,20},{28,24},{1,29},{... | collective-permute-start | bytes 196616 | tf_op jit(solution)/shard_map/ppermute | solution.py:13
Sparse Core Ops, SparseCore 0:
  30.7 19.9 reduce-scatter.4
  91.1 18.4 reduce-scatter.6
  138.4 16.6 reduce-scatter.8
  157.7 19.3 reduce-scatter.10
where the time goes:
time: 186 us; the launch traced here: 184 us
  matrix products  51.4 us (28%)
  blocking collectives  39.4 us (21%)
  waiting for transfers between devices  36.4 us (20%)
  between operations  19.9 us (11%)
  local copies, waits for them, and re-layouts  19.8 us (11%)
  starting transfers between devices  10.2 us (5%)
  other arithmetic  7.23 us (4%)
    all_gather x2, blocking collectives, body(): lax.all_gather(gradient.astype(jnp.bfloat16), 'head', axis=1, tiled=True)  24.7 us
    reduce_scatter x3, waiting for transfers between devices, body(): lax.psum_scatter(decoder_part, 'head', scatter_dimension=1, tiled=True)  24.2 us
    all_gather x1, blocking collectives, body(): gradient = lax.all_gather(gradient, 'head', axis=1, tiled=True)  14.7 us
    ppermute x8, starting transfers between devices, shifted(): return lax.ppermute(value, axis, pairs)  10 us
    ppermute x8, waiting for transfers between devices, shifted(): return lax.ppermute(value, axis, pairs)  7.54 us
    dot_general x3, matrix products, local_terms(): jnp.einsum('hqk,qhd->khd', attention_low, context_heads, preferred_elemen...  6.98 us
    sub x3, matrix products, local_terms(): expo = jnp.exp(scores - row_max)  6.36 us
    reshape x3, local copies, waits for them, and re-layouts, local_terms(): key_heads = keys.reshape(enc_rows, head_local, HEAD_DIM)  5.37 us
  transfers between devices with their start and end apart: 12, of which 7 were waited for; matrix products, arithmetic and copies ran while one was open for 40% of the time, Pallas kernels for 0%

commit v1 on v0

--- a/solution.py
+++ b/solution.py
@@ -111,7 +111,13 @@
         if tick_index + 1 < TICKS:
             held = shifted(held, "segment", -1)
     carried = lax.psum_scatter(carried, "head", scatter_dimension=1, tiled=True)
-    gradient = lax.all_gather(gradient, "head", axis=1, tiled=True)
+    size = lax.axis_size("head")
+    block, blocks = (gradient, [gradient])
+    for _ in range(size - 1):
+        block = lax.ppermute(block, "head", [(i, (i + 1) % size) for i in range(size)])
+        blocks.insert(0, block)
+    line = jnp.concatenate(blocks, axis=1)
+    gradient = jnp.roll(line, (lax.axis_index("head") + 1) * gradient.shape[1], axis=1)
     return (gradient[None], carried[None])
 
 

time: 186 us -> 199 us (1.070)
  waiting for transfers between devices: 36.4 us -> 62.4 us
  blocking collectives: 39.4 us -> 24.7 us
  starting transfers between devices: 10.2 us -> 12.7 us
    ppermute x0 -> x3, waiting for transfers between devices: none -> 17.5 us  [body(): lax.ppermute(block, 'head', [(i, (i + 1) % size) for i in range(size)])]
    all_gather x1 -> x0, blocking collectives: 14.7 us -> none  [body(): gradient = lax.all_gather(gradient, 'head', axis=1, tiled=True)]
    reduce_scatter x1, waiting for transfers between devices: 4.63 us -> 14.2 us  [body(): carried = lax.psum_scatter(carried, 'head', scatter_dimension=1, tiled=True)]
    ppermute x8, waiting for transfers between devices: 7.54 us -> 1.8 us  [shifted(): return lax.ppermute(value, axis, pairs)]
    reduce_scatter x3, waiting for transfers between devices: 24.2 us -> 28.8 us  [body(): lax.psum_scatter(decoder_part, 'head', scatter_dimension=1, tiled=True)]
    ppermute x8, starting transfers between devices: 10 us -> 12.5 us  [shifted(): return lax.ppermute(value, axis, pairs)]
    unnamed x45 -> x53, local copies, waits for them, and re-layouts: 4.67 us -> 4.5 us
  transfers between devices with their start and end apart: 12 -> 15, of which waited for: 7 -> 8; matrix products, arithmetic and copies ran while one was open for 40% -> 37% of each run, Pallas kernels for 0% -> 0%
where the time goes in v1:
time: 199 us; the launch traced here: 198 us
  waiting for transfers between devices  62.4 us (31%)
  matrix products  50.5 us (25%)
  blocking collectives  24.7 us (12%)
  local copies, waits for them, and re-layouts  20.4 us (10%)
  between operations  20 us (10%)
  starting transfers between devices  12.7 us (6%)
  other arithmetic  7.28 us (4%)
    reduce_scatter x3, waiting for transfers between devices, body(): lax.psum_scatter(decoder_part, 'head', scatter_dimension=1, tiled=True)  28.8 us
    all_gather x2, blocking collectives, body(): lax.all_gather(gradient.astype(jnp.bfloat16), 'head', axis=1, tiled=True)  24.7 us
    ppermute x3, waiting for transfers between devices, body(): lax.ppermute(block, 'head', [(i, (i + 1) % size) for i in range(size)])  17.5 us
    reduce_scatter x1, waiting for transfers between devices, body(): carried = lax.psum_scatter(carried, 'head', scatter_dimension=1, tiled=True)  14.2 us
    ppermute x8, starting transfers between devices, shifted(): return lax.ppermute(value, axis, pairs)  12.5 us
    dot_general x3, matrix products, local_terms(): jnp.einsum('hqk,qhd->khd', attention_low, context_heads, preferred_elemen...  7.01 us
    sub x3, matrix products, local_terms(): expo = jnp.exp(scores - row_max)  6.36 us
    reshape x3, local copies, waits for them, and re-layouts, local_terms(): key_heads = keys.reshape(enc_rows, head_local, HEAD_DIM)  5.36 us
  transfers between devices with their start and end apart: 15, of which 8 were waited for; matrix products, arithmetic and copies ran while one was open for 37% of the time, Pallas kernels for 0%

profile of v1, /device:TPU:0, one launch (start us, length us, event | category | flops | bytes accessed | tf_op | source)
XLA Modules:
  0.0 197.9 jit_solution(13779317488252456091)
XLA Ops:
  7.2 3.4 %collective-permute-start.1 = (bf16[128,512]{1,0:T(8,128)(2,1)}, bf16[128,512]{1,0:T(8,128)(2,1)}, u32[]{:S(2)}, u32[]{:S(2)}) collective-permute-start(bf16[128,512]{1,0:T(8,128)(2,1)} %bitcast.204), channel_id=1, source_target_pairs={{0,28},{4,0},{8,4},{12,8},{16,12},{20,16},{24,20},{28,24},{1,29},{... | collective-permute-start | bytes 393224 | tf_op jit(solution)/shard_map/ppermute | solution.py:13
  12.6 1.4 fusion.66
  15.3 1.2 convolution_convert_fusion.19
  16.8 2.2 %convolution_convert_fusion.18 = bf16[128,1024]{1,0:T(8,128)(2,1)} fusion(bf16[1,1024,512]{2,1,0:T(8,128)(2,1)S(1)} %copy-done.3, f32[1,128,512]{2,1,0:T(8,128)} %param.10), kind=kOutput, calls=%fused_computation.30 | convolution fusion | flops 134414336 | bytes 1572864 | tf_op jit(solution)/shard_map/qe,ie->qi/dot_general | solution.py:38
  19.0 1.8 copy.53
  20.8 1.0 convolution_convert_fusion.20
  21.9 1.8 copy.51
  23.7 1.0 fusion.9
  24.7 2.1 %fusion.68 = (f32[8,128]{1,0:T(8,128)S(1)}, f32[8,128,128]{1,2,0:T(8,128)}) fusion(bf16[128,8,128]{0,2,1:T(8,128)(2,1)S(1)} %bitcast.192, bf16[128,8,128]{0,2,1:T(8,128)(2,1)} %bitcast.195, pred[128]{0:T(512)(128)(4,1)S(1)} %iota_compare_fusion.2), kind=kOutput, calls=%fused_computation.118 | convolution fusion | flops 33947776 | bytes 1052800 | tf_op jit(solution)/shard_map/sub | solution.py:35
  26.8 1.5 multiply_reduce_fusion.2
  29.4 1.2 fusion.28
  30.7 2.4 %convolution_convert_fusion.4 = bf16[8,128,128]{2,1,0:T(8,128)(2,1)} fusion(bf16[128,8,128]{0,2,1:T(8,128)(2,1)} %bitcast.208, f32[8,128]{1,0:T(8,128)S(1)} %get-tuple-element.8, bf16[128,8,128]{0,2,1:T(8,128)(2,1)} %bitcast.193, bf16[128,8,128]{0,2,1:T(8,128)(2,1)} %bitcast.196, pred[128]{0:T(512)(128)(4,1)S(1)} %iota_compare_fusion.2), kind=kOutput, calls=%fused_computation.16 | convolution fusion | flops 67765376 | bytes 1052800 | tf_op jit(solution)/shard_map/hqk,qhd->khd/dot_general | solution.py:59
  33.1 1.9 convolution_convert_fusion.5
  35.0 1.4 fusion.35
  36.5 2.2 %convolution_add_fusion.2 = f32[128,512]{1,0:T(8,128)} fusion(f32[128,512]{1,0:T(8,128)S(1)} %fusion.35, bf16[128,1024]{0,1:T(8,128)(2,1)} %bitcast.206, bf16[1,512,1024]{2,1,0:T(8,128)(2,1)S(1)} %copy-done.2), kind=kOutput, calls=%fused_computation.39 | convolution fusion | flops 134283264 | bytes 1835008 | tf_op jit(solution)/shard_map/ki,ei->ke/dot_general | solution.py:67
  38.7 1.5 fusion.60
  44.0 1.9 convolution_convert_fusion.9
  46.6 1.9 convolution_convert_fusion.14
  49.2 1.1 copy.58
  50.3 1.9 copy.55
  52.8 1.9 convolution_convert_fusion.15
  54.7 1.8 copy.54
  56.5 2.2 %fusion.69 = (f32[8,128]{1,0:T(8,128)S(1)}, f32[8,128,128]{1,2,0:T(8,128)}) fusion(bf16[128,8,128]{0,2,1:T(8,128)(2,1)} %bitcast.186, bf16[128,8,128]{0,2,1:T(8,128)(2,1)} %bitcast.189, pred[128]{0:T(512)(128)(4,1)S(1)} %iota_compare_fusion.1), kind=kOutput, calls=%fused_computation.119 | convolution fusion | flops 33947776 | bytes 1052800 | tf_op jit(solution)/shard_map/sub | solution.py:35
  59.3 1.9 fusion.10
  63.2 1.8 copy.57
  64.9 2.1 %fusion.70 = (f32[8,128]{1,0:T(8,128)S(1)}, f32[8,128,128]{1,2,0:T(8,128)}) fusion(bf16[128,8,128]{0,2,1:T(8,128)(2,1)S(1)} %bitcast.180, bf16[128,8,128]{0,2,1:T(8,128)(2,1)} %bitcast.183, pred[128]{0:T(512)(128)(4,1)S(1)} %iota_compare_fusion), kind=kOutput, calls=%fused_computation.120 | convolution fusion | flops 33947776 | bytes 1052800 | tf_op jit(solution)/shard_map/sub | solution.py:35
  68.0 2.7 %collective-permute-start = (f32[128,128]{1,0:T(8,128)S(1)}, f32[128,128]{1,0:T(8,128)S(1)}, u32[]{:S(2)}, u32[]{:S(2)}) collective-permute-start(f32[128,128]{1,0:T(8,128)S(1)} %bitcast_add_fusion.1), channel_id=1, source_target_pairs={{0,28},{4,0},{8,4},{12,8},{16,12},{20,16},{24,20},{28,24},{1,29},{... | collective-permute-start | bytes 196616 | tf_op jit(solution)/shard_map/ppermute | solution.py:13
  70.7 1.0 fusion.11
  73.3 12.5 %all_gather.6 = bf16[128,512]{1,0:T(8,128)(2,1)S(1)} all-gather(bf16[128,128]{1,0:T(8,128)(2,1)S(1)} %convert_element_type.131), channel_id=1, replica_groups=mesh['segment'=8,'head'=4] {'head'}, dimensions={1}, use_global_device_ids=true | all-gather | bytes 163840 | tf_op jit(solution)/shard_map/all_gather | solution.py:94
  87.1 1.5 multiply_reduce_fusion.1
  89.7 1.2 fusion.25
  91.0 2.4 %convolution_convert_fusion.2 = bf16[8,128,128]{2,1,0:T(8,128)(2,1)} fusion(bf16[128,8,128]{0,2,1:T(8,128)(2,1)} %bitcast.210, f32[8,128]{1,0:T(8,128)S(1)} %get-tuple-element.12, bf16[128,8,128]{0,2,1:T(8,128)(2,1)} %bitcast.187, bf16[128,8,128]{0,2,1:T(8,128)(2,1)} %bitcast.190, pred[128]{0:T(512)(128)(4,1)S(1)} %iota_compare_fusion.1), kind=kOutput, calls=%fused_computation.14 | convolution fusion | flops 67765376 | bytes 1052800 | tf_op jit(solution)/shard_map/hqk,qhd->khd/dot_general | solution.py:59
  93.4 1.2 convolution_convert_fusion.3
  95.1 14.4 %reduce-scatter.7.cloned.1.call-done = f32[128,128]{1,0:T(8,128)} async-done(((f32[128,512]{1,0:T(8,128)}), f32[128,128]{1,0:T(8,128)}) %reduce-scatter.7.cloned.1.call-update) | async-done | bytes 65552 | tf_op jit(solution)/shard_map/reduce_scatter | solution.py:106
  110.4 2.3 %fusion.12 = f32[128,512]{1,0:T(8,128)} fusion(f32[128,512]{1,0:T(8,128)} %collective-permute-done.8, f32[128,512]{1,0:T(8,128)S(1)} %fusion.33, bf16[128,1024]{0,1:T(8,128)(2,1)} %bitcast.213, bf16[1,512,1024]{2,1,0:T(8,128)(2,1)S(1)} %copy-done.2), kind=kOutput, calls=%fused_computation.38 | convolution fusion | flops 134348800 | bytes 2097152 | tf_op jit(solution)/shard_map/ki,ei->ke/dot_general | solution.py:67
  112.8 2.5 %collective-permute-start.9 = (f32[128,512]{1,0:T(8,128)}, f32[128,512]{1,0:T(8,128)}, u32[]{:S(2)}, u32[]{:S(2)}) collective-permute-start(f32[128,512]{1,0:T(8,128)} %fusion.12), channel_id=1, source_target_pairs={{0,28},{4,0},{8,4},{12,8},{16,12},{20,16},{24,20},{28,24},{1,29},{... | collective-permute-start | bytes 786440 | tf_op jit(solution)/shard_map/ppermute | solution.py:13
  115.2 12.3 %all_gather.7 = bf16[128,512]{1,0:T(8,128)(2,1)S(1)} all-gather(bf16[128,128]{1,0:T(8,128)(2,1)S(1)} %convert_element_type.139), channel_id=1, replica_groups=mesh['segment'=8,'head'=4] {'head'}, dimensions={1}, use_global_device_ids=true | all-gather | bytes 163840 | tf_op jit(solution)/shard_map/all_gather | solution.py:94
  127.5 1.2 convolution_convert_fusion.8
  128.7 1.8 copy.59
  130.5 2.3 %convolution_convert_fusion = bf16[8,128,128]{2,1,0:T(8,128)(2,1)} fusion(bf16[128,8,128]{0,2,1:T(8,128)(2,1)} %bitcast.211, f32[8,128]{1,0:T(8,128)S(1)} %get-tuple-element.16, bf16[128,8,128]{0,2,1:T(8,128)(2,1)S(1)} %bitcast.181, bf16[128,8,128]{0,2,1:T(8,128)(2,1)} %bitcast.184, pred[128]{0:T(512)(128)(4,1)S(1)} %iota_compare_fusion), kind=kOutput, calls=%fused_computation.12 | convolution fusion | flops 67765376 | bytes 1052800 | tf_op jit(solution)/shard_map/hqk,qhd->khd/dot_general | solution.py:59
  132.8 1.5 multiply_reduce_fusion
  135.6 1.2 fusion.22
  139.2 14.4 %reduce-scatter.9.cloned.1.call-done = f32[128,128]{1,0:T(8,128)} async-done(((f32[128,512]{1,0:T(8,128)}), f32[128,128]{1,0:T(8,128)}) %reduce-scatter.9.cloned.1.call-update) | async-done | bytes 65552 | tf_op jit(solution)/shard_map/reduce_scatter | solution.py:106
  155.6 2.5 %collective-permute-start.10 = (f32[128,512]{1,0:T(8,128)S(1)}, f32[128,512]{1,0:T(8,128)S(1)}, u32[]{:S(2)}, u32[]{:S(2)}) collective-permute-start(f32[128,512]{1,0:T(8,128)S(1)} %add.81), channel_id=1, source_target_pairs={{0,28},{4,0},{8,4},{12,8},{16,12},{20,16},{24,20},{28,24},{1,29},{... | collective-permute-start | bytes 786440 | tf_op jit(solution)/shard_map/ppermute | solution.py:13
  158.1 6.1 %collective-permute-done.5 = f32[128,128]{1,0:T(8,128)S(1)} collective-permute-done((f32[128,128]{1,0:T(8,128)S(1)}, f32[128,128]{1,0:T(8,128)S(1)}, u32[]{:S(2)}, u32[]{:S(2)}) %collective-permute-start.5) | collective-permute-done | bytes 65568 | tf_op jit(solution)/shard_map/ppermute | solution.py:117
  164.1 6.1 %collective-permute-done.6 = f32[128,128]{1,0:T(8,128)S(1)} collective-permute-done((f32[128,128]{1,0:T(8,128)S(1)}, f32[128,128]{1,0:T(8,128)S(1)}, u32[]{:S(2)}, u32[]{:S(2)}) %collective-permute-start.6) | collective-permute-done | bytes 65568 | tf_op jit(solution)/shard_map/ppermute | solution.py:117
  170.9 5.3 %collective-permute-done.7 = f32[128,128]{1,0:T(8,128)S(1)} collective-permute-done((f32[128,128]{1,0:T(8,128)S(1)}, f32[128,128]{1,0:T(8,128)S(1)}, u32[]{:S(2)}, u32[]{:S(2)}) %collective-permute-start.7) | collective-permute-done | bytes 65568 | tf_op jit(solution)/shard_map/ppermute | solution.py:117
  177.1 14.2 %reduce-scatter.11.cloned.1.call-done = f32[128,128]{1,0:T(8,128)} async-done(((f32[128,512]{1,0:T(8,128)}), f32[128,128]{1,0:T(8,128)}) %reduce-scatter.11.cloned.1.call-update) | async-done | bytes 65552 | tf_op jit(solution)/shard_map/reduce_scatter | solution.py:113
  (103 shorter events, 20.7 us)
Async XLA Ops:
  7.2 8.2 %copy-start = (bf16[1,512,1024]{2,1,0:T(8,128)(2,1)S(1)}, bf16[1,512,1024]{2,1,0:T(8,128)(2,1)}, u32[]{:S(2)}) copy-start(bf16[1,512,1024]{2,1,0:T(8,128)(2,1)} %param.16) | copy-start | bytes 3145732
  7.2 3.5 %copy-start.22 = (s32[1,3]{1,0:T(1,128)S(1)}, s32[1,3]{1,0:T(1,128)}, u32[]{:S(2)}) copy-start(s32[1,3]{1,0:T(1,128)} %param.14) | copy-start | bytes 40
  7.2 9.5 %copy-start.3 = (bf16[1,1024,512]{2,1,0:T(8,128)(2,1)S(1)}, bf16[1,1024,512]{2,1,0:T(8,128)(2,1)}, u32[]{:S(2)}) copy-start(bf16[1,1024,512]{2,1,0:T(8,128)(2,1)} %param.19) | copy-start | bytes 3145732
  7.2 59.8 %reduce-scatter.5.cloned.1.call-start = ((), (), s32[]{:S(2)}) async-start(), calls=%async_computation.4 | async-start | bytes 327680 | tf_op jit(solution)/shard_map/reduce_scatter | solution.py:106
  7.2 45.6 %collective-permute-start.1 = (bf16[128,512]{1,0:T(8,128)(2,1)}, bf16[128,512]{1,0:T(8,128)(2,1)}, u32[]{:S(2)}, u32[]{:S(2)}) collective-permute-start(bf16[128,512]{1,0:T(8,128)(2,1)} %bitcast.204), channel_id=1, source_target_pairs={{0,28},{4,0},{8,4},{12,8},{16,12},{20,16},{24,20},{28,24},{1,29},{... | collective-permute-start | bytes 393224 | tf_op jit(solution)/shard_map/ppermute | solution.py:13
  16.7 7.9 %copy-start.10 = (bf16[128,1024]{0,1:T(8,128)(2,1)}, bf16[128,1024]{0,1:T(8,128)(2,1)S(1)}, u32[]{:S(2)}) copy-start(bf16[128,1024]{0,1:T(8,128)(2,1)S(1)} %copy.52) | copy-start | bytes 786436
  16.8 4.1 %copy-start.1 = (bf16[1,512,1024]{2,1,0:T(8,128)(2,1)S(1)}, bf16[1,512,1024]{2,1,0:T(8,128)(2,1)}, u32[]{:S(2)}) copy-start(bf16[1,512,1024]{2,1,0:T(8,128)(2,1)} %param.17) | copy-start | bytes 3145732
  19.0 1.8 copy-start.16
  20.8 2.8 %copy-start.2 = (bf16[1,512,1024]{2,1,0:T(8,128)(2,1)S(1)}, bf16[1,512,1024]{2,1,0:T(8,128)(2,1)}, u32[]{:S(2)}) copy-start(bf16[1,512,1024]{2,1,0:T(8,128)(2,1)} %param.18) | copy-start | bytes 3145732
  26.8 1.5 copy-start.15
  28.3 1.0 copy-start.11
  30.7 78.9 %reduce-scatter.7.cloned.1.call-start = ((), (), s32[]{:S(2)}) async-start(), calls=%async_computation.5 | async-start | bytes 327680 | tf_op jit(solution)/shard_map/reduce_scatter | solution.py:106
  36.5 2.2 %copy-start.21 = (f32[1,128,128]{2,1,0:T(8,128)S(1)}, f32[1,128,128]{2,1,0:T(8,128)}, u32[]{:S(2)}) copy-start(f32[1,128,128]{2,1,0:T(8,128)} %param.12) | copy-start | bytes 196612
  40.2 70.3 %collective-permute-start.8 = (f32[128,512]{1,0:T(8,128)}, f32[128,512]{1,0:T(8,128)}, u32[]{:S(2)}, u32[]{:S(2)}) collective-permute-start(f32[128,512]{1,0:T(8,128)} %fusion.60), channel_id=1, source_target_pairs={{0,28},{4,0},{8,4},{12,8},{16,12},{20,16},{24,20},{28,24},{1,29},{... | collective-permute-start | bytes 786440 | tf_op jit(solution)/shard_map/ppermute | solution.py:13
  50.3 14.7 %copy-start.6 = (bf16[128,1024]{0,1:T(8,128)(2,1)}, bf16[128,1024]{0,1:T(8,128)(2,1)S(1)}, u32[]{:S(2)}) copy-start(bf16[128,1024]{0,1:T(8,128)(2,1)S(1)} %copy.58) | copy-start | bytes 786436
  58.7 3.5 %collective-permute-start.3 = (bf16[128,512]{1,0:T(8,128)(2,1)}, bf16[128,512]{1,0:T(8,128)(2,1)S(1)}, u32[]{:S(2)}, u32[]{:S(2)}) collective-permute-start(bf16[128,512]{1,0:T(8,128)(2,1)} %collective-permute-done.1), channel_id=1, source_target_pairs={{0,28},{4,0},{8,4},{12,8},{16,12},{20,16},{24,20},{28,24},{1,29},{... | collective-permute-start | bytes 393224 | tf_op jit(solution)/shard_map/ppermute | solution.py:13
  67.0 18.7 %copy-start.4 = (bf16[1,1024,512]{2,1,0:T(8,128)(2,1)S(1)}, bf16[1,1024,512]{2,1,0:T(8,128)(2,1)}, u32[]{:S(2)}) copy-start(bf16[1,1024,512]{2,1,0:T(8,128)(2,1)} %param.19) | copy-start | bytes 3145732
  68.0 4.6 %collective-permute-start = (f32[128,128]{1,0:T(8,128)S(1)}, f32[128,128]{1,0:T(8,128)S(1)}, u32[]{:S(2)}, u32[]{:S(2)}) collective-permute-start(f32[128,128]{1,0:T(8,128)S(1)} %bitcast_add_fusion.1), channel_id=1, source_target_pairs={{0,28},{4,0},{8,4},{12,8},{16,12},{20,16},{24,20},{28,24},{1,29},{... | collective-permute-start | bytes 196616 | tf_op jit(solution)/shard_map/ppermute | solution.py:13
  72.6 0.6 copy-start.18
  87.0 1.5 copy-start.14
  88.6 1.0 copy-start.9
  90.9 62.7 %reduce-scatter.9.cloned.1.call-start = ((), (), s32[]{:S(2)}) async-start(), calls=%async_computation.6 | async-start | bytes 327680 | tf_op jit(solution)/shard_map/reduce_scatter | solution.py:106
  94.6 14.9 %copy-start.19 = (f32[128,128]{1,0:T(8,128)S(1)}, f32[128,128]{1,0:T(8,128)}, u32[]{:S(2)}) copy-start(f32[128,128]{1,0:T(8,128)} %copy-done.18) | copy-start | bytes 196612
  110.4 4.9 %collective-permute-start.2 = (f32[128,128]{1,0:T(8,128)S(1)}, f32[128,128]{1,0:T(8,128)S(1)}, u32[]{:S(2)}, u32[]{:S(2)}) collective-permute-start(f32[128,128]{1,0:T(8,128)S(1)} %add.69), channel_id=1, source_target_pairs={{0,28},{4,0},{8,4},{12,8},{16,12},{20,16},{24,20},{28,24},{1,29},{... | collective-permute-start | bytes 196616 | tf_op jit(solution)/shard_map/ppermute | solution.py:13
  110.4 17.1 %copy-start.5 = (bf16[1,1024,512]{2,1,0:T(8,128)(2,1)S(1)}, bf16[1,1024,512]{2,1,0:T(8,128)(2,1)}, u32[]{:S(2)}) copy-start(bf16[1,1024,512]{2,1,0:T(8,128)(2,1)} %param.19) | copy-start | bytes 3145732
  112.8 41.8 %collective-permute-start.9 = (f32[128,512]{1,0:T(8,128)}, f32[128,512]{1,0:T(8,128)}, u32[]{:S(2)}, u32[]{:S(2)}) collective-permute-start(f32[128,512]{1,0:T(8,128)} %fusion.12), channel_id=1, source_target_pairs={{0,28},{4,0},{8,4},{12,8},{16,12},{20,16},{24,20},{28,24},{1,29},{... | collective-permute-start | bytes 786440 | tf_op jit(solution)/shard_map/ppermute | solution.py:13
  128.7 1.8 copy-start.7
  132.8 1.5 copy-start.13
  134.4 1.0 copy-start.8
  136.8 0.9 copy-start.12
  136.9 54.5 %reduce-scatter.11.cloned.1.call-start = ((), (), s32[]{:S(2)}) async-start(), calls=%async_computation.7 | async-start | bytes 327680 | tf_op jit(solution)/shard_map/reduce_scatter | solution.py:113
  137.8 0.9 copy-start.17
  154.5 3.6 %collective-permute-start.4 = (f32[128,128]{1,0:T(8,128)S(1)}, f32[128,128]{1,0:T(8,128)S(1)}, u32[]{:S(2)}, u32[]{:S(2)}) collective-permute-start(f32[128,128]{1,0:T(8,128)S(1)} %add.71), channel_id=1, source_target_pairs={{0,28},{4,0},{8,4},{12,8},{16,12},{20,16},{24,20},{28,24},{1,29},{... | collective-permute-start | bytes 196616 | tf_op jit(solution)/shard_map/ppermute | solution.py:13
  155.6 14.6 %collective-permute-start.10 = (f32[128,512]{1,0:T(8,128)S(1)}, f32[128,512]{1,0:T(8,128)S(1)}, u32[]{:S(2)}, u32[]{:S(2)}) collective-permute-start(f32[128,512]{1,0:T(8,128)S(1)} %add.81), channel_id=1, source_target_pairs={{0,28},{4,0},{8,4},{12,8},{16,12},{20,16},{24,20},{28,24},{1,29},{... | collective-permute-start | bytes 786440 | tf_op jit(solution)/shard_map/ppermute | solution.py:13
  158.1 6.1 %collective-permute-start.5 = (f32[128,128]{1,0:T(8,128)S(1)}, f32[128,128]{1,0:T(8,128)S(1)}, u32[]{:S(2)}, u32[]{:S(2)}) collective-permute-start(f32[128,128]{1,0:T(8,128)S(1)} %collective-permute-done.4), channel_id=1, source_target_pairs={{0,1},{1,2},{2,3},{3,0},{4,5},{5,6},{6,7},{7,4},{8,9},{9,10},{10,1... | collective-permute-start | bytes 196616 | tf_op jit(solution)/shard_map/ppermute | solution.py:117
  164.1 6.1 %collective-permute-start.6 = (f32[128,128]{1,0:T(8,128)S(1)}, f32[128,128]{1,0:T(8,128)S(1)}, u32[]{:S(2)}, u32[]{:S(2)}) collective-permute-start(f32[128,128]{1,0:T(8,128)S(1)} %collective-permute-done.5), channel_id=1, source_target_pairs={{0,1},{1,2},{2,3},{3,0},{4,5},{5,6},{6,7},{7,4},{8,9},{9,10},{10,1... | collective-permute-start | bytes 196616 | tf_op jit(solution)/shard_map/ppermute | solution.py:117
  170.2 6.1 %collective-permute-start.7 = (f32[128,128]{1,0:T(8,128)S(1)}, f32[128,128]{1,0:T(8,128)S(1)}, u32[]{:S(2)}, u32[]{:S(2)}) collective-permute-start(f32[128,128]{1,0:T(8,128)S(1)} %collective-permute-done.6), channel_id=1, source_target_pairs={{0,1},{1,2},{2,3},{3,0},{4,5},{5,6},{6,7},{7,4},{8,9},{9,10},{10,1... | collective-permute-start | bytes 196616 | tf_op jit(solution)/shard_map/ppermute | solution.py:117
  170.2 0.7 copy-start.20
Sparse Core Ops, SparseCore 0:
  30.8 19.9 reduce-scatter.4
  91.1 18.4 reduce-scatter.6
  137.0 16.6 reduce-scatter.8
  171.1 20.2 reduce-scatter.10
